TPU v7x, 32 devices: a whole 2x2x4 slice. The times are simulated.
32 devices in a mesh: orbit: 8 (over y, x, core), tile: 4 (over z).
Axes of the slice: x: 2, y: 2, z: 4, core: 2. Of those that a mesh axis runs over, the one named last changes fastest.
Arguments:
- tokens: bfloat16 [32, 256, 1280], P('orbit', 'tile'), may hold values from -6 to 6
- cotangent: bfloat16 [32, 256, 1280], P('orbit', 'tile'), may hold values from -60 to 60
- w_query: bfloat16 [1280, 1280], replicated, may hold values from -0.15625 to 0.15625
- w_key: bfloat16 [1280, 1280], replicated, may hold values from -0.15625 to 0.15625
- w_value: bfloat16 [1280, 1280], replicated, may hold values from -0.15625 to 0.15625
- conv_taps: float32 [3, 1280], replicated, may hold values from 0.3 to 1
- conv_bias: float32 [1280], replicated, may hold values from -2 to 2
Outputs:
- grad_tokens: bfloat16 [32, 256, 1280], P('orbit', 'tile')
All inputs are finite; a program needn't handle non-finite values.
Results may differ from a plain program's by a relative error of at most 0.009.
The roundings to bfloat16 on the way count: a program that leaves them out, or rounds other values in their place, can miss the bound.
Values may be sent and summed in bfloat16 or wider, within the bound.
No kernel may reach another device: no remote copies, remote signals or barrier semaphores. Data moves between devices by JAX's collectives and lax.ppermute only.
A program may use at most 64 MiB of HBM per device.

v0:
```python
import math
import jax
import jax.numpy as jnp
from jax import lax
from jax.sharding import PartitionSpec as P

HEAD_DIM = 64


def mix_whole(tokens, conv_taps, conv_bias):
    source = tokens.astype(jnp.float32)
    mixed = (
        conv_taps[0] * jnp.roll(source, 1, axis=0)
        + conv_taps[1] * source
        + conv_taps[2] * jnp.roll(source, -1, axis=0)
    )
    return (source + mixed + conv_bias).astype(jnp.bfloat16)


def unmix_whole(grad_hidden, conv_taps):
    source = grad_hidden.astype(jnp.float32)
    result = (
        source
        + conv_taps[0] * jnp.roll(source, -1, axis=0)
        + conv_taps[1] * source
        + conv_taps[2] * jnp.roll(source, 1, axis=0)
    )
    return result.astype(jnp.bfloat16)


def project_all(hidden, weights):
    flat_rows = hidden.reshape(-1, hidden.shape[-1])
    return tuple(
        (
            jnp.dot(flat_rows, weight, preferred_element_type=jnp.float32)
            .astype(jnp.bfloat16)
            .reshape(hidden.shape)
            for weight in weights
        )
    )


def back_project(grad_query, grad_key, grad_value, weights):
    full_shape = grad_query.shape
    channels = full_shape[-1]
    total = jnp.dot(
        grad_query.reshape(-1, channels), weights[0].T, preferred_element_type=jnp.float32
    )
    total = total + jnp.dot(
        grad_key.reshape(-1, channels), weights[1].T, preferred_element_type=jnp.float32
    )
    total = total + jnp.dot(
        grad_value.reshape(-1, channels), weights[2].T, preferred_element_type=jnp.float32
    )
    return total.astype(jnp.bfloat16).reshape(full_shape)


def attention_grads(query_rows, key_rows, value_rows, grad_rows):
    frames, tok_count, channels = query_rows.shape
    head_count = channels // HEAD_DIM
    inv_root = 1.0 / math.sqrt(HEAD_DIM)
    shape_heads = (frames, tok_count, head_count, HEAD_DIM)
    q_heads = query_rows.reshape(shape_heads)
    k_heads = key_rows.reshape(shape_heads)
    v_heads = value_rows.reshape(shape_heads)
    g_heads = grad_rows.reshape(shape_heads)
    scores = (
        jnp.einsum("fshd,gshd->shfg", q_heads, k_heads, preferred_element_type=jnp.float32)
        * inv_root
    )
    peak = jnp.max(scores, axis=-1, keepdims=True)
    expo_terms = jnp.exp(scores - peak)
    attn_prob = expo_terms / jnp.sum(expo_terms, axis=-1, keepdims=True)
    prob_low = attn_prob.astype(jnp.bfloat16)
    attn_out = jnp.einsum("shfg,gshd->fshd", prob_low, v_heads, preferred_element_type=jnp.float32)
    row_delta = jnp.sum(g_heads.astype(jnp.float32) * attn_out, axis=-1)
    grad_value = jnp.einsum(
        "shfg,fshd->gshd", prob_low, g_heads, preferred_element_type=jnp.float32
    ).astype(jnp.bfloat16)
    grad_prob = jnp.einsum("fshd,gshd->shfg", g_heads, v_heads, preferred_element_type=jnp.float32)
    d_scores = attn_prob * (grad_prob - jnp.transpose(row_delta, (1, 2, 0))[..., None])
    scores_low = d_scores.astype(jnp.bfloat16)
    grad_query = (
        jnp.einsum("shfg,gshd->fshd", scores_low, k_heads, preferred_element_type=jnp.float32)
        * inv_root
    ).astype(jnp.bfloat16)
    grad_key = (
        jnp.einsum("shfg,fshd->gshd", scores_low, q_heads, preferred_element_type=jnp.float32)
        * inv_root
    ).astype(jnp.bfloat16)
    full_shape = (frames, tok_count, channels)
    return (
        grad_query.reshape(full_shape),
        grad_key.reshape(full_shape),
        grad_value.reshape(full_shape),
    )


def shards(tokens, cotangent, w_query, w_key, w_value, conv_taps, conv_bias):
    frame_rows, tile_rows, channels = tokens.shape
    spatial_all = tile_rows * lax.axis_size("tile")
    grad_f = cotangent.astype(jnp.float32)
    energy = lax.psum(jnp.sum(grad_f * grad_f, axis=(1, 2)), "tile")
    factor = lax.rsqrt(energy / (spatial_all * channels) + 1e-06)
    grad_out = (grad_f * factor[:, None, None]).astype(jnp.bfloat16)
    weights = (w_query, w_key, w_value)
    tokens_all, grad_all = (
        lax.all_to_all(tokens, "orbit", split_axis=1, concat_axis=0, tiled=True),
        lax.all_to_all(grad_out, "orbit", split_axis=1, concat_axis=0, tiled=True),
    )
    hidden_all = mix_whole(tokens_all, conv_taps, conv_bias)
    query_all, key_all, value_all = project_all(hidden_all, weights)
    grad_query, grad_key, grad_value = attention_grads(query_all, key_all, value_all, grad_all)
    grad_hidden = back_project(grad_query, grad_key, grad_value, weights)
    grad_input = unmix_whole(grad_hidden, conv_taps)
    return lax.all_to_all(grad_input, "orbit", split_axis=0, concat_axis=1, tiled=True)


def solution(mesh):
    in_specs = (P("orbit", "tile", None), P("orbit", "tile", None), P(), P(), P(), P(), P())
    out_specs = P("orbit", "tile", None)
    return jax.shard_map(shards, mesh=mesh, in_specs=in_specs, out_specs=out_specs, check_vma=False)
```

profile of v0, /device:TPU:0, one launch (start us, length us, event | category | flops | bytes accessed | tf_op | source)
XLA Modules:
  0.0 110.7 jit_solution(1591019399376523910)
XLA Ops:
  0.0 2.6 %copy.76 = bf16[4,64,1280]{2,0,1:T(4,128)(2,1)} copy(bf16[4,64,1280]{2,1,0:T(8,128)(2,1)} %param.7) | data formatting | bytes 1310720 | tf_op args[0]
  2.9 5.2 %all-to-all-start = ((bf16[4,64,1280]{2,0,1:T(4,128)(2,1)}), bf16[4,64,1280]{2,0,1:T(4,128)(2,1)}, u32[]{:S(2)}, u32[]{:S(2)}) async-start(bf16[4,64,1280]{2,0,1:T(4,128)(2,1)} %copy.76), calls=%async_computation | async-start | bytes 1310720 | tf_op jit(solution)/shard_map/all_to_all | solution.py:108
  8.1 12.4 %psum.7 = f32[4]{0:T(128)S(1)} all-reduce(f32[4]{0:T(128)S(1)} %fusion.10), channel_id=1, replica_groups=mesh['orbit'=8,'tile'=4] {'tile'}, use_global_device_ids=true, to_apply=%region_3.4 | all-reduce | flops 4 | bytes 32 | tf_op jit(solution)/shard_map/psum | solution.py:103
  23.2 4.2 %all-to-all-start.1 = ((bf16[4,64,1280]{2,0,1:T(4,128)(2,1)}), bf16[4,64,1280]{2,0,1:T(4,128)(2,1)}, u32[]{:S(2)}, u32[]{:S(2)}) async-start(bf16[4,64,1280]{2,0,1:T(4,128)(2,1)} %copy.82), calls=%async_computation.1 | async-start | bytes 1310720 | tf_op jit(solution)/shard_map/all_to_all | solution.py:109
  33.5 3.0 %reshape_reshape.18 = bf16[32,8,20,64]{3,2,1,0:T(8,128)(2,1)} reshape(bf16[256,1280]{1,0:T(8,128)(2,1)} %convolution_convert_fusion.2) | data formatting | bytes 1310720 | tf_op jit(solution)/shard_map/reshape;reshape | solution.py:64
  36.4 2.9 %convolution_convert_fusion.1 = bf16[256,1280]{1,0:T(8,128)(2,1)} fusion(bf16[256,1280]{1,0:T(8,128)(2,1)} %copy-done.12, bf16[1280,1280]{1,0:T(8,128)(2,1)S(1)} %copy-done), kind=kOutput, calls=%fused_computation.12 | convolution fusion | flops 839188480 | bytes 4587520 | tf_op jit(solution)/shard_map/dot_general | solution.py:35
  39.4 3.0 %reshape_reshape.19 = bf16[32,8,20,64]{3,2,1,0:T(8,128)(2,1)} reshape(bf16[256,1280]{1,0:T(8,128)(2,1)} %convolution_convert_fusion.1) | data formatting | bytes 1310720 | tf_op jit(solution)/shard_map/reshape;reshape | solution.py:63
  42.3 3.6 %fusion.24 = f32[8,20,32,32]{2,3,1,0:T(8,128)S(1)} fusion(bf16[32,8,20,64]{3,2,1,0:T(8,128)(2,1)} %reshape_reshape.18, bf16[32,8,20,64]{3,2,1,0:T(8,128)(2,1)} %reshape_reshape.19), kind=kOutput, calls=%fused_computation.46 | convolution fusion | flops 20971520 | bytes 1966080 | tf_op jit(solution)/shard_map/fshd,gshd->shfg/dot_general | solution.py:68
  46.0 2.3 %fusion.39 = (f32[8,20,32]{2,1,0:T(8,128)S(1)}, f32[8,20,32,32]{2,3,1,0:T(8,128)}) fusion(f32[8,20,32,32]{2,3,1,0:T(8,128)S(1)} %fusion.24), kind=kOutput, calls=%fused_computation.67 | output fusion | flops 655391 | bytes 1331200 | tf_op jit(solution)/shard_map/sub | solution.py:72
  50.3 3.0 %reshape.30 = bf16[32,8,20,64]{3,2,1,0:T(8,128)(2,1)} reshape(bf16[8,4,8,1280]{3,2,1,0:T(8,128)(2,1)} %bitcast.84) | data formatting | bytes 1310720 | tf_op jit(solution)/shard_map/reshape | solution.py:66
  53.2 4.1 %convolution_convert_fusion = bf16[256,1280]{1,0:T(8,128)(2,1)} fusion(bf16[256,1280]{1,0:T(8,128)(2,1)} %copy-done.12, bf16[1280,1280]{1,0:T(8,128)(2,1)} %param.11), kind=kOutput, calls=%fused_computation.11 | convolution fusion | flops 839188480 | bytes 4587520 | tf_op jit(solution)/shard_map/dot_general | solution.py:35
  57.3 3.0 %reshape_reshape.20 = bf16[32,8,20,64]{3,2,1,0:T(8,128)(2,1)} reshape(bf16[256,1280]{1,0:T(8,128)(2,1)} %convolution_convert_fusion) | data formatting | bytes 1310720 | tf_op jit(solution)/shard_map/reshape;reshape | solution.py:65
  60.3 3.4 %fusion.7 = bf16[32,8,20,64]{3,0,2,1:T(8,128)(2,1)S(1)} fusion(bf16[32,8,20,64]{3,2,1,0:T(8,128)(2,1)} %reshape.30, f32[8,20,32,32]{2,3,1,0:T(8,128)} %get-tuple-element.17, f32[8,20,32]{2,1,0:T(8,128)S(1)} %get-tuple-element.16), kind=kOutput, calls=%fused_computation.19 | convolution fusion | flops 21626880 | bytes 1986560 | tf_op jit(solution)/shard_map/shfg,fshd->gshd/dot_general | solution.py:77
  64.3 2.1 %fusion.1 = f32[32,8,20]{0,2,1:T(8,128)S(1)} fusion(bf16[32,8,20,64]{3,2,1,0:T(8,128)(2,1)S(1)} %copy-done.11, bf16[32,8,20,64]{3,2,1,0:T(8,128)(2,1)S(1)} %copy-done.10, f32[8,20,32,32]{2,3,1,0:T(8,128)S(1)} %copy-done.6, f32[8,20,32]{2,1,0:T(8,128)S(1)} %get-tuple-element.16), kind=kOutput, calls=%fused_computation.4 | convolution fusion | flops 22277120 | bytes 2007040 | tf_op jit(solution)/shard_map/shfg,gshd->fshd/dot_general | solution.py:75
  66.4 2.1 %multiply_convert_fusion.2 = bf16[8,20,32,32]{2,3,1,0:T(8,128)(2,1)S(1)} fusion(f32[8,20,32]{2,1,0:T(8,128)S(1)} %bitcast.85, bf16[32,8,20,64]{3,2,1,0:T(8,128)(2,1)S(1)} %copy-done.11, f32[8,20,32,32]{2,3,1,0:T(8,128)S(1)} %copy-done.6, f32[8,20,32]{2,1,0:T(8,128)S(1)} %get-tuple-element.16, bf16[32,8,20,64]{3,2,1,0:T(8,128)(2,1)S(1)} %copy-done.10), kind=kOutput, calls=%fused_computation.7 | convolution fusion | flops 21626880 | bytes 2334720 | tf_op jit(solution)/shard_map/fshd,gshd->shfg/dot_general | solution.py:80
  68.5 2.0 %fusion.9 = bf16[32,8,20,64]{3,0,2,1:T(8,128)(2,1)} fusion(bf16[8,20,32,32]{2,3,1,0:T(8,128)(2,1)S(1)} %multiply_convert_fusion.2, bf16[32,8,20,64]{3,2,1,0:T(8,128)(2,1)S(1)} %copy-done.2), kind=kOutput, calls=%fused_computation.21 | convolution fusion | flops 21626880 | bytes 1638400 | tf_op jit(solution)/shard_map/shfg,fshd->gshd/dot_general | solution.py:88
  70.5 2.3 %fusion.8 = bf16[32,8,20,64]{3,0,2,1:T(8,128)(2,1)} fusion(bf16[8,20,32,32]{2,3,1,0:T(8,128)(2,1)S(1)} %multiply_convert_fusion.2, bf16[32,8,20,64]{3,2,1,0:T(8,128)(2,1)S(1)} %copy-done.1), kind=kOutput, calls=%fused_computation.20 | convolution fusion | flops 21626880 | bytes 1638400 | tf_op jit(solution)/shard_map/shfg,gshd->fshd/dot_general | solution.py:84
  74.5 2.7 %reshape_reshape.23 = bf16[256,1280]{1,0:T(8,128)(2,1)} reshape(bf16[32,8,20,64]{3,2,1,0:T(8,128)(2,1)} %copy.96) | data formatting | bytes 1310720 | tf_op jit(solution)/shard_map/reshape;reshape | solution.py:53
  77.3 3.0 %copy.94 = bf16[32,8,20,64]{3,2,1,0:T(8,128)(2,1)} copy(bf16[32,8,20,64]{3,0,2,1:T(8,128)(2,1)} %fusion.9) | data formatting | bytes 1310720 | tf_op jit(solution)/shard_map/convert_element_type | solution.py:90
  80.3 2.8 %reshape_reshape.22 = bf16[256,1280]{1,0:T(8,128)(2,1)} reshape(bf16[32,8,20,64]{3,2,1,0:T(8,128)(2,1)} %copy.94) | data formatting | bytes 1310720 | tf_op jit(solution)/shard_map/reshape;reshape | solution.py:50
  83.0 3.0 %copy.92 = bf16[32,8,20,64]{3,2,1,0:T(8,128)(2,1)} copy(bf16[32,8,20,64]{3,0,2,1:T(8,128)(2,1)} %fusion.8) | data formatting | bytes 1310720 | tf_op jit(solution)/shard_map/convert_element_type | solution.py:86
  86.1 2.7 %reshape_reshape.21 = bf16[256,1280]{1,0:T(8,128)(2,1)} reshape(bf16[32,8,20,64]{3,2,1,0:T(8,128)(2,1)} %copy.92) | data formatting | bytes 1310720 | tf_op jit(solution)/shard_map/reshape;reshape | solution.py:47
  88.8 2.3 %fusion.40 = f32[256,1280]{1,0:T(8,128)S(1)} fusion(bf16[256,1280]{1,0:T(8,128)(2,1)} %reshape_reshape.21, bf16[1280,1280]{1,0:T(8,128)(2,1)S(1)} %copy-done), kind=kOutput, calls=%fused_computation.68 | convolution fusion | flops 838860800 | bytes 5242880 | tf_op jit(solution)/shard_map/dot_general | solution.py:46
  94.8 15.0 %all_to_all.42 = bf16[32,8,1280]{2,1,0:T(8,128)(2,1)S(1)} all-to-all(bf16[32,8,1280]{2,1,0:T(8,128)(2,1)S(1)} %fusion.22), channel_id=1, replica_groups=mesh['orbit'=8,'tile'=4] {'orbit'}, dimensions={0} | all-to-all | bytes 1310720 | tf_op jit(solution)/shard_map/all_to_all | solution.py:116
  (51 shorter events, 17.7 us)
Async XLA Ops:
  0.0 36.4 %copy-start = (bf16[1280,1280]{1,0:T(8,128)(2,1)S(1)}, bf16[1280,1280]{1,0:T(8,128)(2,1)}, u32[]{:S(2)}) copy-start(bf16[1280,1280]{1,0:T(8,128)(2,1)} %param.9) | copy-start | bytes 9830404
  0.0 2.6 %copy-start.7 = (bf16[4,64,1280]{2,1,0:T(8,128)(2,1)S(1)}, bf16[4,64,1280]{2,1,0:T(8,128)(2,1)}, u32[]{:S(2)}) copy-start(bf16[4,64,1280]{2,1,0:T(8,128)(2,1)} %param.8) | copy-start | bytes 1966084
  2.9 20.3 %all-to-all-start = ((bf16[4,64,1280]{2,0,1:T(4,128)(2,1)}), bf16[4,64,1280]{2,0,1:T(4,128)(2,1)}, u32[]{:S(2)}, u32[]{:S(2)}) async-start(bf16[4,64,1280]{2,0,1:T(4,128)(2,1)} %copy.76), calls=%async_computation | async-start | bytes 1310720 | tf_op jit(solution)/shard_map/all_to_all | solution.py:108
  20.5 2.6 %copy-start.13 = (f32[3,1280]{1,0:T(4,128)S(1)}, f32[3,1280]{1,0:T(4,128)}, u32[]{:S(2)}) copy-start(f32[3,1280]{1,0:T(4,128)} %param.12) | copy-start | bytes 46084
  23.2 25.1 %all-to-all-start.1 = ((bf16[4,64,1280]{2,0,1:T(4,128)(2,1)}), bf16[4,64,1280]{2,0,1:T(4,128)(2,1)}, u32[]{:S(2)}, u32[]{:S(2)}) async-start(bf16[4,64,1280]{2,0,1:T(4,128)(2,1)} %copy.82), calls=%async_computation.1 | async-start | bytes 1310720 | tf_op jit(solution)/shard_map/all_to_all | solution.py:109
  28.7 0.7 copy-start.14
  29.4 2.2 %copy-start.3 = (bf16[1280,1280]{1,0:T(8,128)(2,1)S(1)}, bf16[1280,1280]{1,0:T(8,128)(2,1)}, u32[]{:S(2)}) copy-start(bf16[1280,1280]{1,0:T(8,128)(2,1)} %param.10) | copy-start | bytes 9830404
  29.8 0.8 copy-start.12
  60.3 3.4 %copy-start.6 = (f32[8,20,32,32]{2,3,1,0:T(8,128)S(1)}, f32[8,20,32,32]{2,3,1,0:T(8,128)}, u32[]{:S(2)}) copy-start(f32[8,20,32,32]{2,3,1,0:T(8,128)} %get-tuple-element.17) | copy-start | bytes 1966084
  60.3 3.5 %copy-start.10 = (bf16[32,8,20,64]{3,2,1,0:T(8,128)(2,1)S(1)}, bf16[32,8,20,64]{3,2,1,0:T(8,128)(2,1)}, u32[]{:S(2)}) copy-start(bf16[32,8,20,64]{3,2,1,0:T(8,128)(2,1)} %reshape.30) | copy-start | bytes 1966084
  60.3 3.9 %copy-start.11 = (bf16[32,8,20,64]{3,2,1,0:T(8,128)(2,1)S(1)}, bf16[32,8,20,64]{3,2,1,0:T(8,128)(2,1)}, u32[]{:S(2)}) copy-start(bf16[32,8,20,64]{3,2,1,0:T(8,128)(2,1)} %reshape_reshape.20) | copy-start | bytes 1966084
  66.4 2.1 %copy-start.2 = (bf16[32,8,20,64]{3,2,1,0:T(8,128)(2,1)S(1)}, bf16[32,8,20,64]{3,2,1,0:T(8,128)(2,1)}, u32[]{:S(2)}) copy-start(bf16[32,8,20,64]{3,2,1,0:T(8,128)(2,1)} %reshape_reshape.19) | copy-start | bytes 1966084
  68.5 2.1 %copy-start.1 = (bf16[32,8,20,64]{3,2,1,0:T(8,128)(2,1)S(1)}, bf16[32,8,20,64]{3,2,1,0:T(8,128)(2,1)}, u32[]{:S(2)}) copy-start(bf16[32,8,20,64]{3,2,1,0:T(8,128)(2,1)} %reshape_reshape.18) | copy-start | bytes 1966084
  88.8 2.3 %copy-start.4 = (bf16[1280,1280]{1,0:T(8,128)(2,1)S(1)}, bf16[1280,1280]{1,0:T(8,128)(2,1)}, u32[]{:S(2)}) copy-start(bf16[1280,1280]{1,0:T(8,128)(2,1)} %param.10) | copy-start | bytes 9830404
  88.8 2.3 %copy-start.9 = (bf16[256,1280]{1,0:T(8,128)(2,1)S(1)}, bf16[256,1280]{1,0:T(8,128)(2,1)}, u32[]{:S(2)}) copy-start(bf16[256,1280]{1,0:T(8,128)(2,1)} %reshape_reshape.22) | copy-start | bytes 1966084
  91.1 1.9 %copy-start.5 = (bf16[1280,1280]{1,0:T(8,128)(2,1)S(1)}, bf16[1280,1280]{1,0:T(8,128)(2,1)}, u32[]{:S(2)}) copy-start(bf16[1280,1280]{1,0:T(8,128)(2,1)} %param.11) | copy-start | bytes 9830404
  91.1 2.1 %copy-start.8 = (bf16[256,1280]{1,0:T(8,128)(2,1)S(1)}, bf16[256,1280]{1,0:T(8,128)(2,1)}, u32[]{:S(2)}) copy-start(bf16[256,1280]{1,0:T(8,128)(2,1)} %reshape_reshape.23) | copy-start | bytes 1966084
where the time goes:
time: 111 us
  local copies, waits for them, and re-layouts  39 us (35%)
  matrix products  28.8 us (26%)
  blocking collectives  27.5 us (25%)
  starting transfers between devices  9.41 us (8%)
  other arithmetic  5.8 us (5%)
    all_to_all x1, blocking collectives, shards(): lax.all_to_all(grad_input, 'orbit', split_axis=0, concat_axis=1, tiled=True)  15 us
    psum x1, blocking collectives, shards(): energy = lax.psum(jnp.sum(grad_f * grad_f, axis=(1, 2)), 'tile')  12.4 us
    dot_general x3, matrix products, project_all(): jnp.dot(flat_rows, weight, preferred_element_type=jnp.float32)  8.88 us
    unnamed x31, local copies, waits for them, and re-layouts  6.42 us
    all_to_all x1, starting transfers between devices, shards(): lax.all_to_all(tokens, 'orbit', split_axis=1, concat_axis=0, tiled=True)  5.2 us
    all_to_all x1, starting transfers between devices, shards(): lax.all_to_all(grad_out, 'orbit', split_axis=1, concat_axis=0, tiled=True)  4.21 us
    dot_general x1, matrix products, attention_grads(): jnp.einsum('fshd,gshd->shfg', q_heads, k_heads, preferred_element_type=jn...  3.62 us
    dot_general x1, matrix products, attention_grads(): jnp.einsum('shfg,fshd->gshd', prob_low, g_heads, preferred_element_type=j...  3.35 us
  transfers between devices with their start and end apart: 2, of which 0 were waited for; matrix products, arithmetic and copies ran while one was open for 19% of the time, Pallas kernels for 0%

commit v1 on v0

--- a/solution.py
+++ b/solution.py
@@ -100,7 +100,9 @@
     frame_rows, tile_rows, channels = tokens.shape
     spatial_all = tile_rows * lax.axis_size("tile")
     grad_f = cotangent.astype(jnp.float32)
-    energy = lax.psum(jnp.sum(grad_f * grad_f, axis=(1, 2)), "tile")
+    block = jnp.sum(grad_f * grad_f, axis=(1, 2))
+    shards_2 = lax.all_gather(block, "tile")
+    energy = jnp.sum(shards_2, axis=0)
     factor = lax.rsqrt(energy / (spatial_all * channels) + 1e-06)
     grad_out = (grad_f * factor[:, None, None]).astype(jnp.bfloat16)
     weights = (w_query, w_key, w_value)

time: 111 us -> 114 us (1.027)
    psum x1 -> x0, blocking collectives: 12.4 us -> none  [shards(): energy = lax.psum(jnp.sum(grad_f * grad_f, axis=(1, 2)), 'tile')]
    unnamed x0 -> x1, blocking collectives: none -> 12.4 us
    unnamed x31 -> x34, local copies, waits for them, and re-layouts: 6.42 us -> 7.25 us
  transfers between devices with their start and end apart: 2 -> 2, of which waited for: 0 -> 0; matrix products, arithmetic and copies ran while one was open for 19% -> 21% of each run, Pallas kernels for 0% -> 0%
where the time goes in v1:
time: 114 us; the launch traced here: 113 us
  local copies, waits for them, and re-layouts  39.9 us (35%)
  matrix products  28.7 us (25%)
  blocking collectives  27.4 us (24%)
  starting transfers between devices  9.55 us (8%)
  other arithmetic  6.91 us (6%)
    all_to_all x1, blocking collectives, shards(): lax.all_to_all(grad_input, 'orbit', split_axis=0, concat_axis=1, tiled=True)  15 us
    unnamed x1, blocking collectives  12.4 us
    dot_general x3, matrix products, project_all(): jnp.dot(flat_rows, weight, preferred_element_type=jnp.float32)  8.87 us
    unnamed x34, local copies, waits for them, and re-layouts  7.25 us
    all_to_all x1, starting transfers between devices, shards(): lax.all_to_all(tokens, 'orbit', split_axis=1, concat_axis=0, tiled=True)  5.33 us
    all_to_all x1, starting transfers between devices, shards(): lax.all_to_all(grad_out, 'orbit', split_axis=1, concat_axis=0, tiled=True)  4.22 us
    dot_general x1, matrix products, attention_grads(): jnp.einsum('fshd,gshd->shfg', q_heads, k_heads, preferred_element_type=jn...  3.62 us
    dot_general x1, matrix products, attention_grads(): jnp.einsum('shfg,fshd->gshd', prob_low, g_heads, preferred_element_type=j...  3.35 us
  transfers between devices with their start and end apart: 2, of which 0 were waited for; matrix products, arithmetic and copies ran while one was open for 21% of the time, Pallas kernels for 0%

profile of v1, /device:TPU:0, one launch (start us, length us, event | category | flops | bytes accessed | tf_op | source)
XLA Modules:
  0.0 113.4 jit_solution(10136315706134964401)
XLA Ops:
  0.0 2.6 %copy.76 = bf16[4,64,1280]{2,0,1:T(4,128)(2,1)} copy(bf16[4,64,1280]{2,1,0:T(8,128)(2,1)} %param.7) | data formatting | bytes 1310720 | tf_op args[0]
  2.6 5.3 %all-to-all-start = ((bf16[4,64,1280]{2,0,1:T(4,128)(2,1)}), bf16[4,64,1280]{2,0,1:T(4,128)(2,1)}, u32[]{:S(2)}, u32[]{:S(2)}) async-start(bf16[4,64,1280]{2,0,1:T(4,128)(2,1)} %copy.76), calls=%async_computation | async-start | bytes 1310720 | tf_op jit(solution)/shard_map/all_to_all | solution.py:110
  10.7 12.4 %all-reduce = f32[16]{0:T(128)S(1)} all-reduce(f32[16]{0:T(128)S(1)} %dynamic-update-slice), channel_id=2, replica_groups=mesh['orbit'=8,'tile'=4] {'tile'}, use_global_device_ids=true, to_apply=%add | all-reduce | flops 16 | bytes 128
  26.0 4.2 %all-to-all-start.1 = ((bf16[4,64,1280]{2,0,1:T(4,128)(2,1)}), bf16[4,64,1280]{2,0,1:T(4,128)(2,1)}, u32[]{:S(2)}, u32[]{:S(2)}) async-start(bf16[4,64,1280]{2,0,1:T(4,128)(2,1)} %copy.82), calls=%async_computation.1 | async-start | bytes 1310720 | tf_op jit(solution)/shard_map/all_to_all | solution.py:111
  36.2 3.0 %reshape_reshape.18 = bf16[32,8,20,64]{3,2,1,0:T(8,128)(2,1)} reshape(bf16[256,1280]{1,0:T(8,128)(2,1)} %convolution_convert_fusion.2) | data formatting | bytes 1310720 | tf_op jit(solution)/shard_map/reshape;reshape | solution.py:64
  39.2 2.9 %convolution_convert_fusion.1 = bf16[256,1280]{1,0:T(8,128)(2,1)} fusion(bf16[256,1280]{1,0:T(8,128)(2,1)} %copy-done.11, bf16[1280,1280]{1,0:T(8,128)(2,1)S(1)} %copy-done), kind=kOutput, calls=%fused_computation.12 | convolution fusion | flops 839188480 | bytes 4587520 | tf_op jit(solution)/shard_map/dot_general | solution.py:35
  42.2 3.0 %reshape_reshape.19 = bf16[32,8,20,64]{3,2,1,0:T(8,128)(2,1)} reshape(bf16[256,1280]{1,0:T(8,128)(2,1)} %convolution_convert_fusion.1) | data formatting | bytes 1310720 | tf_op jit(solution)/shard_map/reshape;reshape | solution.py:63
  45.1 3.6 %fusion.24 = f32[8,20,32,32]{2,3,1,0:T(8,128)S(1)} fusion(bf16[32,8,20,64]{3,2,1,0:T(8,128)(2,1)} %reshape_reshape.18, bf16[32,8,20,64]{3,2,1,0:T(8,128)(2,1)} %reshape_reshape.19), kind=kOutput, calls=%fused_computation.46 | convolution fusion | flops 20971520 | bytes 1966080 | tf_op jit(solution)/shard_map/fshd,gshd->shfg/dot_general | solution.py:68
  48.7 2.3 %fusion.39 = (f32[8,20,32]{2,1,0:T(8,128)S(1)}, f32[8,20,32,32]{2,3,1,0:T(8,128)}) fusion(f32[8,20,32,32]{2,3,1,0:T(8,128)S(1)} %fusion.24), kind=kOutput, calls=%fused_computation.67 | output fusion | flops 655391 | bytes 1331200 | tf_op jit(solution)/shard_map/sub | solution.py:72
  53.0 3.0 %reshape.34 = bf16[32,8,20,64]{3,2,1,0:T(8,128)(2,1)} reshape(bf16[8,4,8,1280]{3,2,1,0:T(8,128)(2,1)} %bitcast.85) | data formatting | bytes 1310720 | tf_op jit(solution)/shard_map/reshape | solution.py:66
  56.0 4.1 %convolution_convert_fusion = bf16[256,1280]{1,0:T(8,128)(2,1)} fusion(bf16[256,1280]{1,0:T(8,128)(2,1)} %copy-done.11, bf16[1280,1280]{1,0:T(8,128)(2,1)} %param.11), kind=kOutput, calls=%fused_computation.11 | convolution fusion | flops 839188480 | bytes 4587520 | tf_op jit(solution)/shard_map/dot_general | solution.py:35
  60.1 3.0 %reshape_reshape.20 = bf16[32,8,20,64]{3,2,1,0:T(8,128)(2,1)} reshape(bf16[256,1280]{1,0:T(8,128)(2,1)} %convolution_convert_fusion) | data formatting | bytes 1310720 | tf_op jit(solution)/shard_map/reshape;reshape | solution.py:65
  63.1 3.4 %fusion.7 = bf16[32,8,20,64]{3,0,2,1:T(8,128)(2,1)S(1)} fusion(bf16[32,8,20,64]{3,2,1,0:T(8,128)(2,1)} %reshape.34, f32[8,20,32,32]{2,3,1,0:T(8,128)} %get-tuple-element.17, f32[8,20,32]{2,1,0:T(8,128)S(1)} %get-tuple-element.16), kind=kOutput, calls=%fused_computation.19 | convolution fusion | flops 21626880 | bytes 1986560 | tf_op jit(solution)/shard_map/shfg,fshd->gshd/dot_general | solution.py:77
  67.0 2.1 %fusion.1 = f32[32,8,20]{0,2,1:T(8,128)S(1)} fusion(bf16[32,8,20,64]{3,2,1,0:T(8,128)(2,1)S(1)} %copy-done.10, bf16[32,8,20,64]{3,2,1,0:T(8,128)(2,1)S(1)} %copy-done.9, f32[8,20,32,32]{2,3,1,0:T(8,128)S(1)} %copy-done.6, f32[8,20,32]{2,1,0:T(8,128)S(1)} %get-tuple-element.16), kind=kOutput, calls=%fused_computation.4 | convolution fusion | flops 22277120 | bytes 2007040 | tf_op jit(solution)/shard_map/shfg,gshd->fshd/dot_general | solution.py:75
  69.2 2.1 %multiply_convert_fusion.2 = bf16[8,20,32,32]{2,3,1,0:T(8,128)(2,1)S(1)} fusion(f32[8,20,32]{2,1,0:T(8,128)S(1)} %bitcast.86, bf16[32,8,20,64]{3,2,1,0:T(8,128)(2,1)S(1)} %copy-done.10, f32[8,20,32,32]{2,3,1,0:T(8,128)S(1)} %copy-done.6, f32[8,20,32]{2,1,0:T(8,128)S(1)} %get-tuple-element.16, bf16[32,8,20,64]{3,2,1,0:T(8,128)(2,1)S(1)} %copy-done.9), kind=kOutput, calls=%fused_computation.7 | convolution fusion | flops 21626880 | bytes 2334720 | tf_op jit(solution)/shard_map/fshd,gshd->shfg/dot_general | solution.py:80
  71.2 2.0 %fusion.9 = bf16[32,8,20,64]{3,0,2,1:T(8,128)(2,1)} fusion(bf16[8,20,32,32]{2,3,1,0:T(8,128)(2,1)S(1)} %multiply_convert_fusion.2, bf16[32,8,20,64]{3,2,1,0:T(8,128)(2,1)S(1)} %copy-done.2), kind=kOutput, calls=%fused_computation.21 | convolution fusion | flops 21626880 | bytes 1638400 | tf_op jit(solution)/shard_map/shfg,fshd->gshd/dot_general | solution.py:88
  73.3 2.3 %fusion.8 = bf16[32,8,20,64]{3,0,2,1:T(8,128)(2,1)} fusion(bf16[8,20,32,32]{2,3,1,0:T(8,128)(2,1)S(1)} %multiply_convert_fusion.2, bf16[32,8,20,64]{3,2,1,0:T(8,128)(2,1)S(1)} %copy-done.1), kind=kOutput, calls=%fused_computation.20 | convolution fusion | flops 21626880 | bytes 1638400 | tf_op jit(solution)/shard_map/shfg,gshd->fshd/dot_general | solution.py:84
  77.2 2.7 %reshape_reshape.23 = bf16[256,1280]{1,0:T(8,128)(2,1)} reshape(bf16[32,8,20,64]{3,2,1,0:T(8,128)(2,1)} %copy.96) | data formatting | bytes 1310720 | tf_op jit(solution)/shard_map/reshape;reshape | solution.py:53
  80.0 3.0 %copy.94 = bf16[32,8,20,64]{3,2,1,0:T(8,128)(2,1)} copy(bf16[32,8,20,64]{3,0,2,1:T(8,128)(2,1)} %fusion.9) | data formatting | bytes 1310720 | tf_op jit(solution)/shard_map/convert_element_type | solution.py:90
  83.0 2.8 %reshape_reshape.22 = bf16[256,1280]{1,0:T(8,128)(2,1)} reshape(bf16[32,8,20,64]{3,2,1,0:T(8,128)(2,1)} %copy.94) | data formatting | bytes 1310720 | tf_op jit(solution)/shard_map/reshape;reshape | solution.py:50
  85.8 3.0 %copy.92 = bf16[32,8,20,64]{3,2,1,0:T(8,128)(2,1)} copy(bf16[32,8,20,64]{3,0,2,1:T(8,128)(2,1)} %fusion.8) | data formatting | bytes 1310720 | tf_op jit(solution)/shard_map/convert_element_type | solution.py:86
  88.8 2.7 %reshape_reshape.21 = bf16[256,1280]{1,0:T(8,128)(2,1)} reshape(bf16[32,8,20,64]{3,2,1,0:T(8,128)(2,1)} %copy.92) | data formatting | bytes 1310720 | tf_op jit(solution)/shard_map/reshape;reshape | solution.py:47
  91.5 2.3 %fusion.40 = f32[256,1280]{1,0:T(8,128)S(1)} fusion(bf16[256,1280]{1,0:T(8,128)(2,1)} %reshape_reshape.21, bf16[1280,1280]{1,0:T(8,128)(2,1)S(1)} %copy-done), kind=kOutput, calls=%fused_computation.68 | convolution fusion | flops 838860800 | bytes 5242880 | tf_op jit(solution)/shard_map/dot_general | solution.py:46
  97.5 15.0 %all_to_all.42 = bf16[32,8,1280]{2,1,0:T(8,128)(2,1)S(1)} all-to-all(bf16[32,8,1280]{2,1,0:T(8,128)(2,1)S(1)} %fusion.22), channel_id=1, replica_groups=mesh['orbit'=8,'tile'=4] {'orbit'}, dimensions={0} | all-to-all | bytes 1310720 | tf_op jit(solution)/shard_map/all_to_all | solution.py:118
  (56 shorter events, 19.7 us)
Async XLA Ops:
  0.0 39.2 %copy-start = (bf16[1280,1280]{1,0:T(8,128)(2,1)S(1)}, bf16[1280,1280]{1,0:T(8,128)(2,1)}, u32[]{:S(2)}) copy-start(bf16[1280,1280]{1,0:T(8,128)(2,1)} %param.9) | copy-start | bytes 9830404
  2.6 6.7 %copy-start.14 = (u32[32]{0:T(128)S(1)}, u32[32]{0:T(128)}, u32[]{:S(2)}) copy-start(u32[32]{0:T(128)} %constant.16) | copy-start | bytes 388
  2.6 23.4 %all-to-all-start = ((bf16[4,64,1280]{2,0,1:T(4,128)(2,1)}), bf16[4,64,1280]{2,0,1:T(4,128)(2,1)}, u32[]{:S(2)}, u32[]{:S(2)}) async-start(bf16[4,64,1280]{2,0,1:T(4,128)(2,1)} %copy.76), calls=%async_computation | async-start | bytes 1310720 | tf_op jit(solution)/shard_map/all_to_all | solution.py:110
  23.3 2.7 %copy-start.12 = (f32[3,1280]{1,0:T(4,128)S(1)}, f32[3,1280]{1,0:T(4,128)}, u32[]{:S(2)}) copy-start(f32[3,1280]{1,0:T(4,128)} %param.12) | copy-start | bytes 46084
  26.0 25.1 %all-to-all-start.1 = ((bf16[4,64,1280]{2,0,1:T(4,128)(2,1)}), bf16[4,64,1280]{2,0,1:T(4,128)(2,1)}, u32[]{:S(2)}, u32[]{:S(2)}) async-start(bf16[4,64,1280]{2,0,1:T(4,128)(2,1)} %copy.82), calls=%async_computation.1 | async-start | bytes 1310720 | tf_op jit(solution)/shard_map/all_to_all | solution.py:111
  31.5 0.7 copy-start.13
  32.2 2.2 %copy-start.3 = (bf16[1280,1280]{1,0:T(8,128)(2,1)S(1)}, bf16[1280,1280]{1,0:T(8,128)(2,1)}, u32[]{:S(2)}) copy-start(bf16[1280,1280]{1,0:T(8,128)(2,1)} %param.10) | copy-start | bytes 9830404
  32.6 0.8 copy-start.11
  63.1 3.4 %copy-start.6 = (f32[8,20,32,32]{2,3,1,0:T(8,128)S(1)}, f32[8,20,32,32]{2,3,1,0:T(8,128)}, u32[]{:S(2)}) copy-start(f32[8,20,32,32]{2,3,1,0:T(8,128)} %get-tuple-element.17) | copy-start | bytes 1966084
  63.1 3.5 %copy-start.9 = (bf16[32,8,20,64]{3,2,1,0:T(8,128)(2,1)S(1)}, bf16[32,8,20,64]{3,2,1,0:T(8,128)(2,1)}, u32[]{:S(2)}) copy-start(bf16[32,8,20,64]{3,2,1,0:T(8,128)(2,1)} %reshape.34) | copy-start | bytes 1966084
  63.1 3.9 %copy-start.10 = (bf16[32,8,20,64]{3,2,1,0:T(8,128)(2,1)S(1)}, bf16[32,8,20,64]{3,2,1,0:T(8,128)(2,1)}, u32[]{:S(2)}) copy-start(bf16[32,8,20,64]{3,2,1,0:T(8,128)(2,1)} %reshape_reshape.20) | copy-start | bytes 1966084
  69.1 2.1 %copy-start.2 = (bf16[32,8,20,64]{3,2,1,0:T(8,128)(2,1)S(1)}, bf16[32,8,20,64]{3,2,1,0:T(8,128)(2,1)}, u32[]{:S(2)}) copy-start(bf16[32,8,20,64]{3,2,1,0:T(8,128)(2,1)} %reshape_reshape.19) | copy-start | bytes 1966084
  71.2 2.0 %copy-start.1 = (bf16[32,8,20,64]{3,2,1,0:T(8,128)(2,1)S(1)}, bf16[32,8,20,64]{3,2,1,0:T(8,128)(2,1)}, u32[]{:S(2)}) copy-start(bf16[32,8,20,64]{3,2,1,0:T(8,128)(2,1)} %reshape_reshape.18) | copy-start | bytes 1966084
  91.5 2.3 %copy-start.4 = (bf16[1280,1280]{1,0:T(8,128)(2,1)S(1)}, bf16[1280,1280]{1,0:T(8,128)(2,1)}, u32[]{:S(2)}) copy-start(bf16[1280,1280]{1,0:T(8,128)(2,1)} %param.10) | copy-start | bytes 9830404
  91.5 2.3 %copy-start.8 = (bf16[256,1280]{1,0:T(8,128)(2,1)S(1)}, bf16[256,1280]{1,0:T(8,128)(2,1)}, u32[]{:S(2)}) copy-start(bf16[256,1280]{1,0:T(8,128)(2,1)} %reshape_reshape.22) | copy-start | bytes 1966084
  93.9 1.9 %copy-start.5 = (bf16[1280,1280]{1,0:T(8,128)(2,1)S(1)}, bf16[1280,1280]{1,0:T(8,128)(2,1)}, u32[]{:S(2)}) copy-start(bf16[1280,1280]{1,0:T(8,128)(2,1)} %param.11) | copy-start | bytes 9830404
  93.9 2.1 %copy-start.7 = (bf16[256,1280]{1,0:T(8,128)(2,1)S(1)}, bf16[256,1280]{1,0:T(8,128)(2,1)}, u32[]{:S(2)}) copy-start(bf16[256,1280]{1,0:T(8,128)(2,1)} %reshape_reshape.23) | copy-start | bytes 1966084
